TPU v7x, 256 devices: a whole 4x4x8 slice. The times are simulated.
256 devices in a mesh: dp: 32 (over z, x_hi, core), slab: 8 (over y, x_lo).
Axes of the slice: x: 4 (x_hi: 2, x_lo: 2; x = x_hi * 2 + x_lo), y: 4, z: 8, core: 2. Of those that a mesh axis runs over, the one named last changes fastest.
Arguments:
- point_feats: bfloat16 [32, 128, 64, 128], P('dp', 'slab'), may hold values from -6 to 6
- point_coords: bfloat16 [32, 128, 3, 128], P('dp', 'slab'), may hold values from 0 to 1
- slot_block: int32 [32, 8, 8, 4], P('dp', 'slab'), may hold values from 0 to 15
- slot_cell: int32 [32, 8, 8, 4], P('dp', 'slab'), may hold values from 0 to 2047, as said below
- slot_count: int32 [32, 8, 8], P('dp', 'slab'), may hold values from 1 to 4, as said below
- cotangent: float32 [32, 16, 16, 16, 128], P('dp', 'slab'), may hold values from -6 to 6
- offset_map: float32 [64, 3], replicated, may hold values from -12 to 12
- offset_bias: float32 [64], replicated, may hold values from -4 to 4
- kernel_mix: bfloat16 [64, 64, 64], replicated, may hold values from -0.75 to 0.75
- lift_weight: bfloat16 [64, 64], replicated, may hold values from -0.75 to 0.75
Outputs:
- spectral_grad: float32 [64, 16, 16, 16, 128], P('dp', 'slab')
Inputs may be any that keep to these rules, and one draw needn't show every extreme that they name: `slot_cell`: cell row of a slot on its receiving slab index. `slot_count`: in every sample one receiving slab index, drawn from the seed, gets 4 live slots from every sending slab index.
All inputs are finite; a program needn't handle non-finite values.
Results may differ from a plain program's by a relative error of at most 0.0031.
Values may be sent and summed in bfloat16 or wider, within the bound.
A program may use at most 64 MiB of HBM per device.

v0:
```python
import math

import jax
import jax.numpy as jnp
from jax import lax
from jax.sharding import PartitionSpec as P

GX = 128
GY = 128
GZ = 128
BP = 128


def mix_blocks(feats, kernel_mix):
    return jnp.einsum(
        "mcp,hcd->mhpd", feats, kernel_mix, preferred_element_type=jnp.float32
    ).astype(jnp.bfloat16)


def kernel_terms(mixed_feats, coords, cell_x, cell_y, offset_map, offset_bias):
    pos_z = (jnp.arange(GZ).astype(jnp.float32) + 0.5) / GZ
    pos_x = (cell_x.astype(jnp.float32) + 0.5) / GX
    pos_y = (cell_y.astype(jnp.float32) + 0.5) / GY
    coef_x = offset_map[:, 0][None, :, None]
    coef_y = offset_map[:, 1][None, :, None]
    coef_z = offset_map[:, 2][None, :, None]
    cell_part = (
        coef_x * pos_x[:, None, None]
        + coef_y * pos_y[:, None, None]
        + coef_z * pos_z[None, None, :]
    )
    points_f = coords.astype(jnp.float32)
    point_part = (
        coef_x * points_f[:, 0][:, None, :]
        + coef_y * points_f[:, 1][:, None, :]
        + coef_z * points_f[:, 2][:, None, :]
    )
    weights = jax.nn.relu(
        cell_part[:, :, :, None] - point_part[:, :, None, :] + offset_bias[None, :, None, None]
    ).astype(jnp.bfloat16)
    slot_sum = jnp.einsum(
        "mhzp,mhpd->mzd", weights, mixed_feats, preferred_element_type=jnp.float32
    ) * (1.0 / BP)
    return slot_sum.reshape(slot_sum.shape[0], -1)


def live_terms(source, coords, cell_x, cell_y, is_live, kernel_args):
    offset_map, offset_bias, kernel_mix = kernel_args
    slot_total = is_live.shape[0]
    width = GZ * kernel_mix.shape[2]
    order = jnp.argsort(jnp.where(is_live, 0, 1).astype(jnp.int32), stable=True)
    inverse = jnp.argsort(order)
    live_total = jnp.sum(is_live.astype(jnp.int32))
    group_size = math.gcd(slot_total, 4)
    groups = slot_total // group_size
    group_ids = jnp.arange(groups, dtype=jnp.int32)

    def regroup(values):
        return values[order].reshape((groups, group_size) + values.shape[1:])

    def slot_group(group_args):
        group_id, src_rows, coord_rows, row_x, row_y = group_args

        def compute():
            mixed = mix_blocks(src_rows, kernel_mix)
            return kernel_terms(mixed, coord_rows, row_x, row_y, offset_map, offset_bias)

        def skipped():
            return jnp.zeros((group_size, width), jnp.float32)

        return lax.cond(group_id * group_size < live_total, compute, skipped)

    result = lax.map(
        slot_group, (group_ids, regroup(source), regroup(coords), regroup(cell_x), regroup(cell_y))
    )
    return result.reshape(slot_total, width)[inverse]


def spectral_modes(
    slot_terms, cell_ids, cell_x, cell_y, lift_weight, mode_count, channels, spec_scale
):
    slot_total = cell_ids.shape[0]
    is_live = cell_ids >= 0
    same_cell = (cell_ids[:, None] == cell_ids[None, :]) & is_live[None, :]
    slot_index = jnp.arange(slot_total, dtype=jnp.int32)
    before = same_cell & (slot_index[None, :] < slot_index[:, None])
    leader = (is_live & jnp.logical_not(jnp.any(before, axis=1))).astype(jnp.float32)
    summed = jnp.dot(
        same_cell.astype(jnp.float32),
        slot_terms,
        precision=lax.Precision.HIGHEST,
        preferred_element_type=jnp.float32,
    )
    latent = summed.astype(jnp.bfloat16).reshape(slot_total * GZ, channels)
    lifted = jax.nn.gelu(jnp.dot(latent, lift_weight, preferred_element_type=jnp.float32)).reshape(
        slot_total, GZ, channels
    )
    lifted = lifted * leader[:, None, None]
    cells_z = jnp.arange(GZ, dtype=jnp.int32)
    mode_freq = jnp.arange(mode_count, dtype=jnp.int32)
    z_turn = jnp.mod(cells_z[:, None] * mode_freq[None, :], GZ).astype(jnp.float32) * (
        2.0 * math.pi / GZ
    )
    z_table = jnp.concatenate([jnp.cos(z_turn), -jnp.sin(z_turn)], axis=1)
    z_modes = jnp.einsum(
        "nzc,zk->nkc",
        lifted,
        z_table,
        precision=lax.Precision.HIGHEST,
        preferred_element_type=jnp.float32,
    )
    real_z = z_modes[:, :mode_count].reshape(slot_total, mode_count * channels)
    imag_z = z_modes[:, mode_count:].reshape(slot_total, mode_count * channels)
    signed = jnp.where(mode_freq < mode_count // 2, mode_freq, mode_freq - mode_count)
    step_x = jnp.mod(cell_x[:, None].astype(jnp.int32) * signed[None, :], GX).astype(jnp.float32)
    step_y = jnp.mod(cell_y[:, None].astype(jnp.int32) * signed[None, :], GY).astype(jnp.float32)
    phase_angle = (step_x[:, :, None] / GX + step_y[:, None, :] / GY) * (2.0 * math.pi)
    phase_angle = phase_angle.reshape(slot_total, mode_count * mode_count)
    cos_part = jnp.cos(phase_angle)
    sin_part = -jnp.sin(phase_angle)
    contract = (((0,), (0,)), ((), ()))
    high = lax.Precision.HIGHEST
    real_x = lax.dot_general(
        cos_part, real_z, contract, precision=high, preferred_element_type=jnp.float32
    ) - lax.dot_general(
        sin_part, imag_z, contract, precision=high, preferred_element_type=jnp.float32
    )
    imag_x = lax.dot_general(
        cos_part, imag_z, contract, precision=high, preferred_element_type=jnp.float32
    ) + lax.dot_general(
        sin_part, real_z, contract, precision=high, preferred_element_type=jnp.float32
    )
    out_shape = (mode_count, mode_count, mode_count, channels)
    return (
        jnp.concatenate([real_x.reshape(out_shape), imag_x.reshape(out_shape)], axis=3) * spec_scale
    )


def per_device(
    point_feats,
    point_coords,
    slot_block,
    slot_cell,
    slot_count,
    cotangent,
    offset_map,
    offset_bias,
    kernel_mix,
    lift_weight,
):
    slab_count = lax.axis_size("slab")
    slab_index = lax.axis_index("slab")
    channels = point_feats.shape[2]
    mode_count = cotangent.shape[2]
    capacity = slot_block.shape[3]
    planes = GX // slab_count
    kernel_args = (offset_map, offset_bias, kernel_mix)
    block_picks = slot_block[0, 0]
    coords_sent = point_coords[0][block_picks]
    slot_order = jnp.arange(capacity, dtype=jnp.int32)
    is_live = slot_order[None, :] < slot_count[0, 0][:, None]
    cell_tags = jnp.where(is_live, slot_cell[0, 0], -1)
    feats_sent = point_feats[0][block_picks]
    feats_in = lax.all_to_all(feats_sent, "slab", split_axis=0, concat_axis=0, tiled=True)
    coords_in = lax.all_to_all(coords_sent, "slab", split_axis=0, concat_axis=0, tiled=True)
    tags_in = lax.all_to_all(cell_tags, "slab", split_axis=0, concat_axis=0, tiled=True)
    tag_shape = tags_in.shape
    flat_tags = tags_in.reshape(-1)
    cell_id = jnp.maximum(flat_tags, 0)
    row_x = slab_index * planes + cell_id // GY
    row_y = cell_id % GY
    flat_terms = live_terms(
        feats_in.reshape((-1,) + feats_in.shape[2:]),
        coords_in.reshape((-1,) + coords_in.shape[2:]),
        row_x,
        row_y,
        flat_tags >= 0,
        kernel_args,
    )
    slot_terms, tags_in = (flat_terms.reshape(tag_shape + (flat_terms.shape[1],)), tags_in)
    flat_slots = slot_terms.reshape(slab_count * capacity, -1)
    flat_tags = tags_in.reshape(-1)
    cell_id = jnp.maximum(flat_tags, 0)
    spec_scale = 1.0 / math.sqrt(GZ * slab_count * slab_count * capacity)
    partial_modes = spectral_modes(
        flat_slots,
        flat_tags,
        slab_index * planes + cell_id // GY,
        cell_id % GY,
        lift_weight,
        mode_count,
        channels,
        spec_scale,
    )
    local_modes = lax.psum_scatter(partial_modes, "slab", scatter_dimension=0, tiled=True)
    real_modes = local_modes[..., :channels]
    imag_modes = local_modes[..., channels:]
    grad_real = cotangent[0, ..., :channels]
    grad_imag = cotangent[0, ..., channels:]
    left_side = jnp.concatenate([grad_real, grad_imag], axis=3)
    right_side = jnp.concatenate([grad_imag, -grad_real], axis=3)
    part_real = jnp.moveaxis(real_modes, 3, 0)
    part_imag = jnp.moveaxis(imag_modes, 3, 0)
    return lax.psum_scatter(
        part_real[..., None] * left_side[None] + part_imag[..., None] * right_side[None],
        "dp",
        scatter_dimension=0,
        tiled=True,
    )


def solution(mesh):
    placed = (
        P("dp", "slab", None, None),
        P("dp", "slab", None, None),
        P("dp", "slab", None, None),
        P("dp", "slab", None, None),
        P("dp", "slab", None),
        P("dp", "slab", None, None, None),
        P(),
        P(),
        P(),
        P(),
    )
    return jax.shard_map(
        per_device,
        mesh=mesh,
        in_specs=placed,
        out_specs=P("dp", "slab", None, None, None),
        check_vma=False,
    )
```

profile of v0, /device:TPU:3, one launch (start us, length us, event | category | flops | bytes accessed | tf_op | source)
XLA Modules:
  0.0 437.7 jit_solution(8513321495980740915)
XLA Ops:
  6.5 0.7 bitcast_select_fusion
  7.3 0.7 copy.38
  7.9 5.4 %all-to-all-start = ((s32[8,1,4]{2,1,0:T(1,128)}), s32[8,1,4]{2,1,0:T(1,128)S(1)}, u32[]{:S(2)}, u32[]{:S(2)}) async-start(s32[8,1,4]{2,1,0:T(1,128)} %copy.38), calls=%async_computation | async-start | bytes 8192 | tf_op jit(solution)/shard_map/all_to_all | solution.py:166
  13.4 0.7 compare_select_fusion
  14.2 0.7 copy.59
  15.6 0.6 copy.41
  16.2 1.4 gather_fusion.4
  17.6 1.6 copy.45
  19.2 5.2 %all-to-all-start.1 = ((bf16[8,4,3,128]{3,1,2,0:T(4,128)(2,1)}), bf16[8,4,3,128]{3,1,2,0:T(4,128)(2,1)S(1)}, u32[]{:S(2)}, u32[]{:S(2)}) async-start(bf16[8,4,3,128]{3,1,2,0:T(4,128)(2,1)} %copy.41), calls=%async_computation.1 | async-start | bytes 49152 | tf_op jit(solution)/shard_map/all_to_all | solution.py:165
  24.9 1.3 fusion.62
  26.5 1.6 sort.34
  28.1 1.6 sort.35
  29.7 5.2 %all-to-all-start.2 = ((bf16[8,4,64,128]{3,2,1,0:T(8,128)(2,1)}), bf16[8,4,64,128]{3,2,1,0:T(8,128)(2,1)S(1)}, u32[]{:S(2)}, u32[]{:S(2)}) async-start(bf16[8,4,64,128]{3,2,1,0:T(8,128)(2,1)} %bitcast.28), calls=%async_computation.2 | async-start | bytes 1048576 | tf_op jit(solution)/shard_map/all_to_all | solution.py:164
  34.9 0.7 gather_fusion.1
  35.6 0.7 gather_fusion
  37.0 0.6 gather_fusion.3
  37.7 4.1 all-to-all-done.2
  41.8 0.6 gather_fusion.5
  42.5 43.6 %while.10 = (s32[]{:T(128)}, f32[8,4,8192]{2,1,0:T(4,128)}, s32[8]{0:T(128)S(1)}, s32[]{:T(128)}, f32[64,3]{0,1:T(4,128)}, /*index=5*/s32[8,4]{1,0:T(8,128)S(1)}...) while((s32[]{:T(128)}, f32[8,4,8192]{2,1,0:T(4,128)}, ...), condition=%wide.region_5.6_spmd, body=%wide.region_2.5_spmd.sunk | while | flops 824420992 | bytes 2656351 | solution.py:73
  42.5 0.7 dynamic_slice.64
  44.5 7.4 %conditional.2 = (f32[1,4,8192]{2,1,0:T(4,128)S(1)}) conditional(s32[]{:T(128)} %convert_element_type.135, () %tuple.50, (f32[64,3]{0,1:T(4,128)}, s32[8,4]{1,0:T(8,128)S(1)}, s32[]{:T(128)}, s32[8,4]{1,0:T(8,128)S(1)}, bf16[8,4,3,128]{3,1,2,0:T(4,128)(2,1)S(1)}, /*index=5*/f32[64]{0:T(128)}, bf16[8,4,64,128]{3,2,1,0:T(8,128)(2,1)S(1)}, ...), branch_computations={%region_3.3_spmd, %region_4.4_spmd} | conditional | flops 824420992 | bytes 2393460 | solution.py:71
  44.5 0.8 slice_bitcast_fusion.5
  45.7 5.9 %fusion.12 = f32[4,128,64]{1,2,0:T(8,128)S(1)} fusion(f32[64]{0:T(128)} %get-tuple-element.129, f32[4,64,128]{2,1,0:T(8,128)S(1)} %multiply_add_fusion, f32[4,64,128]{2,1,0:T(8,128)S(1)} %broadcast_add_fusion, bf16[64,64,64]{1,2,0:T(8,128)(2,1)S(1)} %get-tuple-element.131, bf16[8,4,64,128]{3,2,1,0:T(8,128)(2,1)S(1)} %get-tuple-element.130, ...), kind=kOutput, calls=%fused_computation.17 | convolution fusion | flops 824213504 | bytes 1507588 | tf_op jit(solution)/shard_map/while/body/eval_jaxpr/cond/branch_1_fun/mhzp,mhpd->mzd/dot_general | solution.py:41
  51.8 0.7 constant_dynamic-update-slice_fusion.2
  52.5 0.7 dynamic_slice.64
  54.5 7.4 %conditional.2 = (f32[1,4,8192]{2,1,0:T(4,128)S(1)}) conditional(s32[]{:T(128)} %convert_element_type.135, () %tuple.50, (f32[64,3]{0,1:T(4,128)}, s32[8,4]{1,0:T(8,128)S(1)}, s32[]{:T(128)}, s32[8,4]{1,0:T(8,128)S(1)}, bf16[8,4,3,128]{3,1,2,0:T(4,128)(2,1)S(1)}, /*index=5*/f32[64]{0:T(128)}, bf16[8,4,64,128]{3,2,1,0:T(8,128)(2,1)S(1)}, ...), branch_computations={%region_3.3_spmd, %region_4.4_spmd} | conditional | flops 824420992 | bytes 2393460 | solution.py:71
  54.5 0.8 slice_bitcast_fusion.5
  55.7 5.9 %fusion.12 = f32[4,128,64]{1,2,0:T(8,128)S(1)} fusion(f32[64]{0:T(128)} %get-tuple-element.129, f32[4,64,128]{2,1,0:T(8,128)S(1)} %multiply_add_fusion, f32[4,64,128]{2,1,0:T(8,128)S(1)} %broadcast_add_fusion, bf16[64,64,64]{1,2,0:T(8,128)(2,1)S(1)} %get-tuple-element.131, bf16[8,4,64,128]{3,2,1,0:T(8,128)(2,1)S(1)} %get-tuple-element.130, ...), kind=kOutput, calls=%fused_computation.17 | convolution fusion | flops 824213504 | bytes 1507588 | tf_op jit(solution)/shard_map/while/body/eval_jaxpr/cond/branch_1_fun/mhzp,mhpd->mzd/dot_general | solution.py:41
  61.9 0.7 constant_dynamic-update-slice_fusion.2
  62.5 0.7 dynamic_slice.64
  64.5 7.4 %conditional.2 = (f32[1,4,8192]{2,1,0:T(4,128)S(1)}) conditional(s32[]{:T(128)} %convert_element_type.135, () %tuple.50, (f32[64,3]{0,1:T(4,128)}, s32[8,4]{1,0:T(8,128)S(1)}, s32[]{:T(128)}, s32[8,4]{1,0:T(8,128)S(1)}, bf16[8,4,3,128]{3,1,2,0:T(4,128)(2,1)S(1)}, /*index=5*/f32[64]{0:T(128)}, bf16[8,4,64,128]{3,2,1,0:T(8,128)(2,1)S(1)}, ...), branch_computations={%region_3.3_spmd, %region_4.4_spmd} | conditional | flops 824420992 | bytes 2393460 | solution.py:71
  64.6 0.8 slice_bitcast_fusion.5
  65.7 5.9 %fusion.12 = f32[4,128,64]{1,2,0:T(8,128)S(1)} fusion(f32[64]{0:T(128)} %get-tuple-element.129, f32[4,64,128]{2,1,0:T(8,128)S(1)} %multiply_add_fusion, f32[4,64,128]{2,1,0:T(8,128)S(1)} %broadcast_add_fusion, bf16[64,64,64]{1,2,0:T(8,128)(2,1)S(1)} %get-tuple-element.131, bf16[8,4,64,128]{3,2,1,0:T(8,128)(2,1)S(1)} %get-tuple-element.130, ...), kind=kOutput, calls=%fused_computation.17 | convolution fusion | flops 824213504 | bytes 1507588 | tf_op jit(solution)/shard_map/while/body/eval_jaxpr/cond/branch_1_fun/mhzp,mhpd->mzd/dot_general | solution.py:41
  71.9 0.7 constant_dynamic-update-slice_fusion.2
  72.5 0.7 dynamic_slice.64
  74.6 0.7 constant_dynamic-update-slice_fusion.2
  75.3 0.7 dynamic_slice.64
  77.3 0.7 constant_dynamic-update-slice_fusion.2
  78.0 0.7 dynamic_slice.64
  80.0 0.7 constant_dynamic-update-slice_fusion.2
  80.6 0.7 dynamic_slice.64
  82.7 0.7 constant_dynamic-update-slice_fusion.2
  83.3 0.7 dynamic_slice.64
  85.4 0.7 constant_dynamic-update-slice_fusion.2
  86.1 1.6 reshape.447
  87.6 0.9 gather_fusion.6
  88.6 0.6 convolution_convert_fusion
  89.2 1.1 reshape.448
  90.9 3.0 convolution_bitcast_fusion
  94.2 1.0 fusion.69
  95.1 1.0 fusion.68
  96.1 1.0 convolution_add_fusion
  97.1 2.0 convolution_subtract_fusion
  99.1 1.7 reshape.452
  100.8 1.9 reshape.453
  102.6 3.6 maximum_multiply_fusion
  106.3 1.0 fusion.66
  107.2 1.2 slice_bitcast_fusion.9
  108.7 90.3 %reduce-scatter.3.cloned.1.call-done = f32[2,16,16,128]{3,2,1,0:T(8,128)} async-done(((f32[16,16,16,128]{3,2,1,0:T(8,128)}), f32[2,16,16,128]{3,2,1,0:T(8,128)}) %reduce-scatter.3.cloned.1.call-update) | async-done | bytes 262160 | tf_op jit(solution)/shard_map/reduce_scatter | solution.py:195
  198.9 1.2 slice_bitcast_fusion.7
  200.1 0.9 copy.47
  201.0 0.9 copy.48
  202.0 11.1 %multiply_add_fusion.2 = f32[64,2,16,16,128]{4,3,2,1,0:T(8,128)} fusion(f32[2,16,16,128]{3,2,1,0:T(8,128)S(1)} %get-tuple-element.220, f32[64,2,16,16]{3,2,1,0:T(8,128)S(1)} %copy.48, f32[2,16,16,128]{3,2,1,0:T(8,128)S(1)} %get-tuple-element.219, f32[64,2,16,16]{3,2,1,0:T(8,128)S(1)} %copy.47), kind=kLoop, calls=%fused_computation.46 | loop fusion | flops 12582912 | bytes 17563648 | tf_op jit(solution)/shard_map/add | solution.py:205
  213.1 217.8 %reduce-scatter.5.cloned.1.call-done = f32[2,2,16,16,128]{4,3,2,1,0:T(8,128)} async-done(((f32[64,2,16,16,128]{4,3,2,1,0:T(8,128)}), f32[2,2,16,16,128]{4,3,2,1,0:T(8,128)}) %reduce-scatter.5.cloned.1.call-update) | async-done | bytes 524304 | tf_op jit(solution)/shard_map/reduce_scatter | solution.py:204
  (81 shorter events, 5.8 us)
Async XLA Ops:
  6.5 9.7 %copy-start = (bf16[1,16,64,128]{3,2,1,0:T(8,128)(2,1)S(1)}, bf16[1,16,64,128]{3,2,1,0:T(8,128)(2,1)}, u32[]{:S(2)}) copy-start(bf16[1,16,64,128]{3,2,1,0:T(8,128)(2,1)} %param.14) | copy-start | bytes 786436
  7.9 11.3 %all-to-all-start = ((s32[8,1,4]{2,1,0:T(1,128)}), s32[8,1,4]{2,1,0:T(1,128)S(1)}, u32[]{:S(2)}, u32[]{:S(2)}) async-start(s32[8,1,4]{2,1,0:T(1,128)} %copy.38), calls=%async_computation | async-start | bytes 8192 | tf_op jit(solution)/shard_map/all_to_all | solution.py:166
  19.2 10.5 %all-to-all-start.1 = ((bf16[8,4,3,128]{3,1,2,0:T(4,128)(2,1)}), bf16[8,4,3,128]{3,1,2,0:T(4,128)(2,1)S(1)}, u32[]{:S(2)}, u32[]{:S(2)}) async-start(bf16[8,4,3,128]{3,1,2,0:T(4,128)(2,1)} %copy.41), calls=%async_computation.1 | async-start | bytes 49152 | tf_op jit(solution)/shard_map/all_to_all | solution.py:165
  29.7 12.1 %all-to-all-start.2 = ((bf16[8,4,64,128]{3,2,1,0:T(8,128)(2,1)}), bf16[8,4,64,128]{3,2,1,0:T(8,128)(2,1)S(1)}, u32[]{:S(2)}, u32[]{:S(2)}) async-start(bf16[8,4,64,128]{3,2,1,0:T(8,128)(2,1)} %bitcast.28), calls=%async_computation.2 | async-start | bytes 1048576 | tf_op jit(solution)/shard_map/all_to_all | solution.py:164
  34.9 164.1 %reduce-scatter.3.cloned.1.call-start = ((), (), s32[]{:S(2)}) async-start(), calls=%async_computation.5 | async-start | bytes 2359296 | tf_op jit(solution)/shard_map/reduce_scatter | solution.py:195
  42.5 47.9 %copy-start.1 = (bf16[64,64]{1,0:T(8,128)(2,1)S(1)}, bf16[64,64]{1,0:T(8,128)(2,1)}, u32[]{:S(2)}) copy-start(bf16[64,64]{1,0:T(8,128)(2,1)} %param.23) | copy-start | bytes 24580
  106.2 324.7 %reduce-scatter.5.cloned.1.call-start = ((), (), s32[]{:S(2)}) async-start(), calls=%async_computation.6 | async-start | bytes 17301504 | tf_op jit(solution)/shard_map/reduce_scatter | solution.py:204
Sparse Core Ops, SparseCore 0:
  106.3 92.5 reduce-scatter.2
  213.2 217.6 reduce-scatter.4
where the time goes:
time: 443 us; the launch traced here: 438 us
  waiting for transfers between devices  312 us (70%)
  local copies, waits for them, and re-layouts  34.8 us (8%)
  matrix products  26.7 us (6%)
  other arithmetic  23.7 us (5%)
  starting transfers between devices  15.7 us (4%)
  between operations  13.6 us (3%)
  loops' own time  11 us (2%)
    reduce_scatter x1, waiting for transfers between devices, per_device(): lax.psum_scatter(part_real[..., None] * left_side[None] + part_imag[...,...  218 us
    reduce_scatter x1, waiting for transfers between devices, per_device(): lax.psum_scatter(partial_modes, 'slab', scatter_dimension=0, tiled=True)  90.3 us
    dot_general x3, matrix products, kernel_terms(): jnp.einsum('mhzp,mhpd->mzd', weights, mixed_feats, preferred_element_type...  17.6 us
    add x1, other arithmetic, per_device(): part_real[..., None] * left_side[None]  11.1 us
    another operation x1, loops' own time, live_terms(): lax.map(slot_group, (group_ids, regroup(source), regroup(coords), regroup...  10.7 us
  transfers between devices with their start and end apart: 5, of which 3 were waited for; matrix products, arithmetic and copies ran while one was open for 4% of the time, Pallas kernels for 0%

commit v1 on v0

v1 whole, which is shorter than its diff:
```python
import math

import jax
import jax.numpy as jnp
import numpy as np
from jax import lax
from jax.experimental import pallas as pl
from jax.experimental.pallas import tpu as pltpu
from jax.sharding import PartitionSpec as P

F32 = jnp.float32
BF16 = jnp.bfloat16
NT = (((1,), (1,)), ((), ()))
VMEM_BYTES = 60 * 2**20


def split(x):
    hi = x.astype(BF16)
    return hi, (x - hi.astype(F32)).astype(BF16)


def dot3(a, b):
    ah, al = a
    bh, bl = b
    out = jnp.dot(ah, bh, preferred_element_type=F32)
    out = out + jnp.dot(al, bh, preferred_element_type=F32)
    return out + jnp.dot(ah, bl, preferred_element_type=F32)


def np_split(x):
    hi = np.asarray(x, np.float32).astype(BF16)
    lo = (np.asarray(x, np.float64) - hi.astype(np.float64)).astype(BF16)
    return hi, lo


def tables():
    z = np.arange(128)
    k = np.arange(16)
    turn = np.mod(z[:, None] * k[None, :], 128) * (2.0 * np.pi / 128)
    z_table = np.tile(np.concatenate([np.cos(turn), -np.sin(turn)], axis=1), (1, 8))
    z_hi, z_lo = np_split(z_table)
    signed = np.where(k < 8, k, k - 16)
    angle = np.mod(signed[:, None] * z[None, :], 128) * (2.0 * np.pi / 128)
    by_x = np.repeat(angle, 16, axis=0)
    by_y = np.tile(angle, (16, 1))
    xy = []
    for part in (np.cos(by_x), np.sin(by_x), np.cos(by_y), np.sin(by_y)):
        xy.append(np.concatenate(np_split(part), axis=1))
    return z_hi, z_lo, np.concatenate(xy, axis=0)


def terms_kernel(blk, cel, cnt, om, feats, coords, mix, coef, lift, out, mixed, tab, base, lifted, live, todo, seen):
    for b in range(16):
        seen[b] = 0

    def scan(n, carry):
        n_live, n_todo = carry
        slab = n // 4
        is_live = (n - slab * 4) < cnt[slab]
        b = blk[n]
        fresh = jnp.logical_and(is_live, seen[b] == 0)
        live[n_live] = n
        todo[n_todo] = b
        seen[b] = jnp.where(is_live, 1, seen[b])
        return n_live + is_live.astype(jnp.int32), n_todo + fresh.astype(jnp.int32)

    n_live, n_todo = lax.fori_loop(0, 32, scan, (jnp.int32(0), jnp.int32(0)))
    lifted[...] = jnp.zeros_like(lifted)
    pos_z = (lax.broadcasted_iota(jnp.int32, (128, 128), 0).astype(F32) + 0.5) * (1.0 / 128)

    def fill(h, carry):
        tab[h] = pos_z * om[h * 3 + 2]
        return carry

    lax.fori_loop(0, 64, fill, 0)

    def mix_pair(i, carry):
        b0 = todo[2 * i]
        b1 = todo[jnp.minimum(2 * i + 1, n_todo - 1)]
        pair = jnp.concatenate([feats[b0], feats[b1]], axis=1)

        def rows(r, carry):
            start = pl.multiple_of(r * 512, 512)
            m = jnp.dot(mix[pl.ds(start, 512), :], pair, preferred_element_type=F32).astype(BF16)
            mixed[b0, pl.ds(start, 512), :] = m[:, :128]
            mixed[b1, pl.ds(start, 512), :] = m[:, 128:]
            return carry

        return lax.fori_loop(0, 8, rows, carry)

    lax.fori_loop(0, (n_todo + 1) // 2, mix_pair, 0)
    coef_x, coef_y, coef_z, bias = (coef[:, c : c + 1] for c in range(4))
    lift_v = lift[...]

    def slot(i, carry):
        n = live[i]
        b = blk[n]
        cell = cel[n]
        x = (n // 4) * 16 + cell // 128
        y = lax.rem(cell, 128)
        pos_x = (x.astype(F32) + 0.5) * (1.0 / 128)
        pos_y = (y.astype(F32) + 0.5) * (1.0 / 128)
        q = coords[b].astype(F32)
        point = coef_x * q[0:1] + coef_y * q[1:2] + coef_z * q[2:3]
        base[...] = (coef_x * pos_x + coef_y * pos_y) + bias - point
        ws, ms = [], []
        for h in range(64):
            w = (tab[h] + base[pl.ds(h, 1), :]).astype(BF16)
            ws.append(jnp.maximum(w, jnp.zeros_like(w)))
            ms.append(mixed[b, h * 64 : (h + 1) * 64, :])
        total = lax.dot_general(
            jnp.concatenate(ws, axis=1), jnp.concatenate(ms, axis=1), NT, preferred_element_type=F32
        )
        hi, lo = split(total.T * (1.0 / 128))
        pre = jnp.dot(lift_v, hi, preferred_element_type=F32) + jnp.dot(lift_v, lo, preferred_element_type=F32)
        lifted[pl.ds(pl.multiple_of(n * 64, 64), 64), :] = pre
        return carry

    lax.fori_loop(0, n_live, slot, 0)
    for e in range(64):
        out[e // 8, e % 8] = lifted[pl.ds(e, 32, stride=64), :].astype(BF16)


def lifted_terms(blk, cel, cnt, om, feats, coords, mix, coef, lift):
    sm = pl.BlockSpec(memory_space=pltpu.SMEM)
    vm = pl.BlockSpec(memory_space=pltpu.VMEM)
    return pl.pallas_call(
        terms_kernel,
        out_shape=jax.ShapeDtypeStruct((8, 8, 32, 128), BF16),
        in_specs=[sm] * 4 + [vm] * 5,
        out_specs=vm,
        scratch_shapes=[
            pltpu.VMEM((16, 4096, 128), BF16),
            pltpu.VMEM((64, 128, 128), F32),
            pltpu.VMEM((64, 128), F32),
            pltpu.VMEM((32 * 64, 128), F32),
            pltpu.SMEM((33,), jnp.int32),
            pltpu.SMEM((33,), jnp.int32),
            pltpu.SMEM((16,), jnp.int32),
        ],
        compiler_params=pltpu.CompilerParams(vmem_limit_bytes=VMEM_BYTES),
        cost_estimate=pl.CostEstimate(flops=4 * 10**9, bytes_accessed=2 * 2**20, transcendentals=0),
        name="slot_terms",
    )(blk, cel, cnt, om, feats, coords, mix, coef, lift)


def modes_value(tag_col, tag_row, terms, z_hi, z_lo, xy):
    lane = lax.broadcasted_iota(jnp.int32, (256, 256), 1)
    row = lax.broadcasted_iota(jnp.int32, (256, 256), 0)
    same = jnp.logical_and(tag_col == tag_row, tag_row >= 0)
    before = jnp.logical_and(same, lane < row)
    early = jnp.max(jnp.where(before, 1.0, 0.0), axis=1, keepdims=True)
    leader = jnp.where(tag_col[:, :1] >= 0, 1.0 - early, 0.0)
    sums = jnp.dot(jnp.where(same, 1.0, 0.0).astype(BF16), terms, preferred_element_type=F32)
    inner = math.sqrt(2.0 / math.pi) * (sums + 0.044715 * (sums * sums * sums))
    acts = (0.5 * leader) * (sums * (1.0 + jnp.tanh(inner)))
    z_lane = lax.broadcasted_iota(jnp.int32, (128, 256), 1) // 32
    zero = jnp.zeros((128, 256), BF16)
    zm = jnp.zeros((256, 256), F32)
    for e in range(8):
        pick = z_lane == e
        zm = zm + dot3(
            split(acts[:, e * 128 : (e + 1) * 128]),
            (jnp.where(pick, z_hi, zero), jnp.where(pick, z_lo, zero)),
        )
    imag_lane = (lane // 16) % 2 == 1
    swapped = jnp.where(imag_lane, pltpu.roll(zm, 16, 1), -pltpu.roll(zm, 240, 1))
    tag = jnp.maximum(tag_row, 0)
    pos = row % 128
    hot_x = jnp.where(pos == tag // 128, 1.0, 0.0).astype(BF16)
    hot_y = jnp.where(pos == tag % 128, 1.0, 0.0).astype(BF16)
    by_x = jnp.dot(xy[:512], hot_x, preferred_element_type=F32)
    by_y = jnp.dot(xy[512:], hot_y, preferred_element_type=F32)
    cos_x, sin_x, cos_y, sin_y = by_x[:256], by_x[256:], by_y[:256], by_y[256:]
    cos_part = cos_x * cos_y - sin_x * sin_y
    sin_part = -(sin_x * cos_y + cos_x * sin_y)
    out = dot3(split(cos_part), split(zm)) + dot3(split(sin_part), split(swapped))
    return out * (1.0 / math.sqrt(32768.0))


def modes_kernel(tag_col, tag_row, terms, z_hi, z_lo, xy, out):
    t = jnp.concatenate(
        [jnp.concatenate([terms[r, e] for r in range(8)], axis=0) for e in range(8)], axis=1
    )
    col = jnp.concatenate([tag_col[...]] * 2, axis=1)
    row = jnp.broadcast_to(tag_row[0:1, :], (256, 256))
    out[...] = modes_value(col, row, t, z_hi[...], z_lo[...], xy[...]).astype(out.dtype)


def kept_modes(tag_col, tag_row, terms):
    z_hi, z_lo, xy = (jnp.asarray(t) for t in tables())
    vm = pl.BlockSpec(memory_space=pltpu.VMEM)
    return pl.pallas_call(
        modes_kernel,
        out_shape=jax.ShapeDtypeStruct((256, 256), BF16),
        in_specs=[vm] * 6,
        out_specs=vm,
        compiler_params=pltpu.CompilerParams(vmem_limit_bytes=VMEM_BYTES),
        name="kept_modes",
    )(tag_col, tag_row, terms, z_hi, z_lo, xy)


def grad_kernel(x, g, out):
    sign = jnp.where(lax.broadcasted_iota(jnp.int32, (16, 128), 1) < 64, 1.0, -1.0)

    def mode_rows(k, carry):
        xk = x[k].astype(F32)
        rows = pl.ds(pl.multiple_of(k * 16, 16), 16)
        acc = [jnp.zeros((16, 128), F32) for _ in range(4)]
        for s in range(32):
            gs = g[s, rows, :].astype(F32)
            for q in range(4):
                acc[q] = acc[q] + xk[q * 16 : (q + 1) * 16, s : s + 1] * gs
        for i in range(2):
            out[i, rows, :] = acc[2 * i] + sign * pltpu.roll(acc[2 * i + 1], 64, 1)
        return carry

    lax.fori_loop(0, 32, mode_rows, 0)


def weight_grad(x, g):
    vm = pl.BlockSpec(memory_space=pltpu.VMEM)
    return pl.pallas_call(
        grad_kernel,
        out_shape=jax.ShapeDtypeStruct((2, 512, 128), F32),
        in_specs=[vm] * 2,
        out_specs=vm,
        compiler_params=pltpu.CompilerParams(vmem_limit_bytes=VMEM_BYTES),
        name="weight_grad",
    )(x, g)


def per_device(
    point_feats, point_coords, slot_block, slot_cell, slot_count, cotangent,
    offset_map, offset_bias, kernel_mix, lift_weight,
):
    grads = cotangent[0].reshape(512, 128).astype(BF16)
    grads_all = lax.all_gather(grads, "dp", axis=0, tiled=False)
    cells = slot_cell[0, 0]
    counts = slot_count[0, 0]
    is_live = jnp.arange(4, dtype=jnp.int32)[None, :] < counts[:, None]
    tags = jnp.where(is_live, jnp.arange(8, dtype=jnp.int32)[:, None] * 2048 + cells, -1).reshape(1, 32)
    tags_in = lax.all_to_all(jnp.broadcast_to(tags, (8, 32)), "slab", 0, 0, tiled=True).reshape(256)
    tag_col = jnp.broadcast_to(tags_in[:, None], (256, 128))
    tag_row = jnp.broadcast_to(tags_in[None, :], (8, 256))
    mix = jnp.transpose(kernel_mix, (0, 2, 1)).reshape(4096, 64)
    coef = jnp.concatenate([offset_map, offset_bias[:, None]], axis=1)
    terms = lifted_terms(
        slot_block.reshape(32), slot_cell.reshape(32), counts, offset_map.reshape(192),
        point_feats[0], point_coords[0], mix, coef, lift_weight.T,
    )
    terms_in = lax.all_to_all(terms, "slab", 0, 0, tiled=True)
    x = kept_modes(tag_col, tag_row, terms_in)
    x = lax.all_to_all(x.reshape(8, 32, 256), "slab", 0, 0, tiled=True)
    x = x.reshape(8, 32, 4, 64).transpose(0, 2, 1, 3).reshape(32, 32, 64)
    x = lax.all_to_all(x, "dp", 0, 0, tiled=True)
    grad = weight_grad(x.transpose(1, 2, 0), grads_all)
    return grad.reshape(2, 2, 16, 16, 128)


def solution(mesh):
    placed = (
        P("dp", "slab", None, None), P("dp", "slab", None, None), P("dp", "slab", None, None),
        P("dp", "slab", None, None), P("dp", "slab", None), P("dp", "slab", None, None, None),
        P(), P(), P(), P(),
    )
    return jax.shard_map(
        per_device,
        mesh=mesh,
        in_specs=placed,
        out_specs=P("dp", "slab", None, None, None),
        check_vma=False,
    )
```

time: 443 us -> 138 us (0.31)
  the two profiles are of different devices: /device:TPU:3 before, /device:TPU:1 now
where the time goes in v1:
time: 138 us; the launch traced here: 137 us
  Pallas kernels  44.4 us (32%)
  blocking collectives  34 us (25%)
  starting transfers between devices  14.3 us (10%)
  local copies, waits for them, and re-layouts  13.9 us (10%)
  between operations  13.4 us (10%)
  waiting for transfers between devices  13.1 us (9%)
  other arithmetic  3.74 us (3%)
    pallas_call x1, Pallas kernels, lifted_terms(): pl.pallas_call(terms_kernel, out_shape=jax.ShapeDtypeStruct((8, 8, 32, 12...  26.9 us
    all_to_all x1, blocking collectives, per_device(): x = lax.all_to_all(x, 'dp', 0, 0, tiled=True)  25 us
    pallas_call x1, Pallas kernels, weight_grad(): pl.pallas_call(grad_kernel, out_shape=jax.ShapeDtypeStruct((2, 512, 128),...  13.3 us
    all_to_all x1, waiting for transfers between devices, per_device(): terms_in = lax.all_to_all(terms, 'slab', 0, 0, tiled=True)  13.1 us
    all_to_all x1, blocking collectives, per_device(): x = lax.all_to_all(x.reshape(8, 32, 256), 'slab', 0, 0, tiled=True)  9 us
    all_to_all x1, starting transfers between devices, per_device(): terms_in = lax.all_to_all(terms, 'slab', 0, 0, tiled=True)  8.34 us
    all_to_all x1, starting transfers between devices, per_device(): lax.all_to_all(jnp.broadcast_to(tags, (8, 32)), 'slab', 0, 0, tiled=True)  5.94 us
    unnamed x11, local copies, waits for them, and re-layouts  5.43 us
  transfers between devices with their start and end apart: 3, of which 1 were waited for; matrix products, arithmetic and copies ran while one was open for 12% of the time, Pallas kernels for 23%

profile of v1, /device:TPU:1, one launch (start us, length us, event | category | flops | bytes accessed | tf_op | source)
XLA Modules:
  0.0 136.9 jit_solution(11442692733931366363)
XLA Ops:
  6.5 0.0 all-gather.2.cloned.1.call-start
  6.5 1.6 %convert_element_type.13 = bf16[1,2,16,16,128]{4,3,2,1,0:T(8,128)(2,1)} convert(f32[1,2,16,16,128]{4,3,2,1,0:T(8,128)} %param.18) | non-fusion elementwise | flops 65536 | bytes 393216 | tf_op jit(solution)/shard_map/convert_element_type | solution.py:237
  8.2 0.0 all-gather.2.cloned.1.call-update
  8.2 0.8 copy.30
  8.9 0.1 squeeze.10.cel
  9.0 0.0 copy-start.1
  9.0 0.7 iota_compare_fusion
  9.8 0.1 lt.26
  9.8 0.1 add.14
  9.9 0.1 add.15
  10.0 0.6 broadcast_in_dim.27
  10.6 5.9 %all-to-all-start = ((s32[8,1,32]{2,1,0:T(1,128)}), s32[8,1,32]{2,1,0:T(1,128)S(1)}, u32[]{:S(2)}, u32[]{:S(2)}) async-start(s32[8,1,32]{2,1,0:T(1,128)} %broadcast_in_dim.27), calls=%async_computation | async-start | bytes 8192 | tf_op jit(solution)/shard_map/all_to_all | solution.py:243
  16.6 2.3 %copy.34 = bf16[64,64,64]{2,1,0:T(8,128)(2,1)} copy(bf16[64,64,64]{1,2,0:T(8,128)(2,1)} %bitcast.19) | data formatting | bytes 1048576 | tf_op jit(solution)/shard_map/transpose | solution.py:246
  18.8 0.8 copy.32
  19.6 0.7 pad_maximum_fusion.1
  20.3 0.7 copy.36.coef
  21.0 0.7 reshape.75.om
  21.7 1.3 copy.39
  23.0 1.4 %copy.35 = bf16[64,64]{0,1:T(8,128)(2,1)} copy(bf16[64,64]{1,0:T(8,128)(2,1)} %param.22) | data formatting | bytes 16384 | tf_op args[9]
  24.5 0.8 copy.31
  25.2 0.6 reshape.74.blk
  25.8 0.0 copy-done.1
  25.8 26.9 %slot_terms.1 = bf16[8,8,32,128]{3,2,1,0:T(8,128)(2,1)} custom-call(s32[32]{0:T(128)} %reshape.74.blk, s32[32]{0:T(128)} %copy-done.1, s32[8]{0:T(128)} %bitcast.29, f32[192]{0:T(256)} %reshape.75.om, bf16[16,64,128]{2,1,0:T(8,128)(2,1)} %bitcast.27, bf16[16,3,128]{2,1,0:T(4,128)(2,1)} %bitcast.24, bf16[4096,64]{1,0:T(8,128)(2,1)} %bitcast.20, ...), custom_call_target="tpu_custom_call" | custom-call | flops 4000000000 | bytes 2097152 | tf_op jit(solution)/shard_map/slot_terms/pallas_call | solution.py:127
  52.7 0.0 all-to-all-done
  52.7 8.3 %all-to-all-start.1 = ((bf16[8,8,32,128]{3,2,1,0:T(8,128)(2,1)}), bf16[8,8,32,128]{3,2,1,0:T(8,128)(2,1)S(1)}, u32[]{:S(2)}, u32[]{:S(2)}) async-start(bf16[8,8,32,128]{3,2,1,0:T(8,128)(2,1)} %slot_terms.1), calls=%async_computation.1 | async-start | bytes 1048576 | tf_op jit(solution)/shard_map/all_to_all | solution.py:252
  61.0 0.5 broadcast.27
  61.6 0.6 reduce.3
  62.2 0.1 broadcast_in_dim.28
  62.3 13.1 %all-to-all-done.1.terms = bf16[8,8,32,128]{3,2,1,0:T(8,128)(2,1)S(1)} async-done(((bf16[8,8,32,128]{3,2,1,0:T(8,128)(2,1)}), bf16[8,8,32,128]{3,2,1,0:T(8,128)(2,1)S(1)}, u32[]{:S(2)}, u32[]{:S(2)}) %all-to-all-start.1) | async-done | bytes 524320 | tf_op jit(solution)/shard_map/all_to_all | solution.py:252
  75.4 0.0 copy-start
  75.4 0.8 broadcast_in_dim.29.tag_col
  76.2 0.6 broadcast_in_dim.30.tag_row
  76.8 0.0 copy-done
  76.8 4.2 %kept_modes.1 = bf16[256,256]{1,0:T(8,128)(2,1)} custom-call(s32[256,128]{1,0:T(8,128)} %broadcast_in_dim.29.tag_col, s32[8,256]{1,0:T(8,128)} %broadcast_in_dim.30.tag_row, bf16[8,8,32,128]{3,2,1,0:T(8,128)(2,1)} %copy-done, bf16[128,256]{1,0:T(8,128)(2,1)} %constant.10.clone.z_hi, bf16[128,256]{1,0:T(8,128)(2,1)} %constant.11.clone.z_lo, ...), custom_call_target="tpu_custom_call" | custom-call | tf_op jit(solution)/shard_map/kept_modes/pallas_call | solution.py:193
  81.0 9.0 %all_to_all.21 = bf16[8,32,256]{2,1,0:T(8,128)(2,1)S(1)} all-to-all(bf16[8,32,256]{2,1,0:T(8,128)(2,1)} %bitcast.23), channel_id=1, replica_groups=mesh['dp'=32,'slab'=8] {'slab'}, dimensions={0} | all-to-all | bytes 262144 | tf_op jit(solution)/shard_map/all_to_all | solution.py:254
  90.0 0.1 fusion
  90.2 0.1 pad_maximum_fusion
  90.2 0.2 reshape.89
  90.4 25.0 %all_to_all.22 = bf16[32,2,1024]{2,1,0:T(2,128)(2,1)S(1)} all-to-all(bf16[32,2,1024]{2,1,0:T(2,128)(2,1)S(1)} %reshape.89), channel_id=1, replica_groups=mesh['dp'=32,'slab'=8] {'dp'}, dimensions={0} | all-to-all | bytes 262144 | tf_op jit(solution)/shard_map/all_to_all | solution.py:256
  115.4 0.2 reshape.90
  115.7 1.2 copy.37
  116.8 0.0 all-gather.2.cloned.1.call-done.g
  116.8 13.3 %weight_grad.1 = f32[2,512,128]{2,1,0:T(8,128)} custom-call(bf16[32,64,32]{2,1,0:T(8,128)(2,1)} %bitcast.18, bf16[32,512,128]{2,1,0:T(8,128)(2,1)} %all-gather.2.cloned.1.call-done.g), custom_call_target="tpu_custom_call" | custom-call | tf_op jit(solution)/shard_map/weight_grad/pallas_call | solution.py:223
  (2 shorter events, 0.0 us)
Async XLA Ops:
  6.5 110.3 %all-gather.2.cloned.1.call-start = ((), (), s32[]{:S(2)}) async-start(), calls=%async_computation.4 | async-start | bytes 4325376 | tf_op jit(solution)/shard_map/all_gather | solution.py:238
  9.0 16.8 %copy-start.1 = (s32[32]{0:T(128)}, s32[32]{0:T(128)S(1)}, u32[]{:S(2)}) copy-start(s32[32]{0:T(128)S(1)} %squeeze.10.cel) | copy-start | bytes 388
  10.6 42.1 %all-to-all-start = ((s32[8,1,32]{2,1,0:T(1,128)}), s32[8,1,32]{2,1,0:T(1,128)S(1)}, u32[]{:S(2)}, u32[]{:S(2)}) async-start(s32[8,1,32]{2,1,0:T(1,128)} %broadcast_in_dim.27), calls=%async_computation | async-start | bytes 8192 | tf_op jit(solution)/shard_map/all_to_all | solution.py:243
  52.7 22.7 %all-to-all-start.1 = ((bf16[8,8,32,128]{3,2,1,0:T(8,128)(2,1)}), bf16[8,8,32,128]{3,2,1,0:T(8,128)(2,1)S(1)}, u32[]{:S(2)}, u32[]{:S(2)}) async-start(bf16[8,8,32,128]{3,2,1,0:T(8,128)(2,1)} %slot_terms.1), calls=%async_computation.1 | async-start | bytes 1048576 | tf_op jit(solution)/shard_map/all_to_all | solution.py:252
  75.4 1.4 %copy-start = (bf16[8,8,32,128]{3,2,1,0:T(8,128)(2,1)}, bf16[8,8,32,128]{3,2,1,0:T(8,128)(2,1)S(1)}, u32[]{:S(2)}) copy-start(bf16[8,8,32,128]{3,2,1,0:T(8,128)(2,1)S(1)} %all-to-all-done.1.terms) | copy-start | bytes 1572868
Sparse Core Ops, SparseCore 0:
  10.1 96.5 all-gather.1

commit v2 on v1

--- a/solution.py
+++ b/solution.py
@@ -49,15 +49,19 @@
     return z_hi, z_lo, np.concatenate(xy, axis=0)
 
 
-def terms_kernel(blk, cel, cnt, om, feats, coords, mix, coef, lift, out, mixed, tab, base, lifted, live, todo, seen):
+def terms_kernel(
+    blk, cel, cnt, om, feats, coords, kmix, coef, bias_ref, lift_ref, cot,
+    out, tags, cot_out, mixed, mix, tab, base, lifted, live, todo, seen,
+):
     for b in range(16):
         seen[b] = 0
 
     def scan(n, carry):
         n_live, n_todo = carry
         slab = n // 4
-        is_live = (n - slab * 4) < cnt[slab]
-        b = blk[n]
+        j = n - slab * 4
+        is_live = j < cnt[slab]
+        b = blk[slab, j]
         fresh = jnp.logical_and(is_live, seen[b] == 0)
         live[n_live] = n
         todo[n_todo] = b
@@ -65,11 +69,22 @@
         return n_live + is_live.astype(jnp.int32), n_todo + fresh.astype(jnp.int32)
 
     n_live, n_todo = lax.fori_loop(0, 32, scan, (jnp.int32(0), jnp.int32(0)))
+    place = lax.broadcasted_iota(jnp.int32, (8, 256), 1) - 32 * lax.axis_index("slab")
+    tag = jnp.zeros((8, 256), F32)
+    for n in range(32):
+        value = jnp.where(n % 4 < cnt[n // 4], (n // 4) * 2048 + cel[n // 4, n % 4], -1).astype(F32)
+        tag = jnp.where(place == n, value, tag)
+    tags[...] = tag
+    for a in range(4):
+        cot_out[a] = cot[a * 128 : (a + 1) * 128, :].T.astype(BF16)
+    for h in range(32):
+        both = jnp.concatenate([kmix[2 * h], kmix[2 * h + 1]], axis=1).astype(F32)
+        mix[h * 128 : (h + 1) * 128, :] = both.T.astype(BF16)
     lifted[...] = jnp.zeros_like(lifted)
     pos_z = (lax.broadcasted_iota(jnp.int32, (128, 128), 0).astype(F32) + 0.5) * (1.0 / 128)
 
     def fill(h, carry):
-        tab[h] = pos_z * om[h * 3 + 2]
+        tab[h] = pos_z * om[h, 2]
         return carry
 
     lax.fori_loop(0, 64, fill, 0)
@@ -89,14 +104,16 @@
         return lax.fori_loop(0, 8, rows, carry)
 
     lax.fori_loop(0, (n_todo + 1) // 2, mix_pair, 0)
-    coef_x, coef_y, coef_z, bias = (coef[:, c : c + 1] for c in range(4))
-    lift_v = lift[...]
+    coef_x, coef_y, coef_z = (coef[:, c : c + 1] for c in range(3))
+    bias = bias_ref[...]
+    lift_v = lift_ref[...].astype(F32).T.astype(BF16)
 
     def slot(i, carry):
         n = live[i]
-        b = blk[n]
-        cell = cel[n]
-        x = (n // 4) * 16 + cell // 128
+        slab = n // 4
+        b = blk[slab, n - slab * 4]
+        cell = cel[slab, n - slab * 4]
+        x = slab * 16 + cell // 128
         y = lax.rem(cell, 128)
         pos_x = (x.astype(F32) + 0.5) * (1.0 / 128)
         pos_y = (y.astype(F32) + 0.5) * (1.0 / 128)
@@ -121,16 +138,21 @@
         out[e // 8, e % 8] = lifted[pl.ds(e, 32, stride=64), :].astype(BF16)
 
 
-def lifted_terms(blk, cel, cnt, om, feats, coords, mix, coef, lift):
+def lifted_terms(*args):
     sm = pl.BlockSpec(memory_space=pltpu.SMEM)
     vm = pl.BlockSpec(memory_space=pltpu.VMEM)
     return pl.pallas_call(
         terms_kernel,
-        out_shape=jax.ShapeDtypeStruct((8, 8, 32, 128), BF16),
-        in_specs=[sm] * 4 + [vm] * 5,
-        out_specs=vm,
+        out_shape=(
+            jax.ShapeDtypeStruct((8, 8, 32, 128), BF16),
+            jax.ShapeDtypeStruct((8, 256), F32),
+            jax.ShapeDtypeStruct((4, 128, 128), BF16),
+        ),
+        in_specs=[sm] * 4 + [vm] * 7,
+        out_specs=(vm, vm, vm),
         scratch_shapes=[
             pltpu.VMEM((16, 4096, 128), BF16),
+            pltpu.VMEM((4096, 64), BF16),
             pltpu.VMEM((64, 128, 128), F32),
             pltpu.VMEM((64, 128), F32),
             pltpu.VMEM((32 * 64, 128), F32),
@@ -139,9 +161,8 @@
             pltpu.SMEM((16,), jnp.int32),
         ],
         compiler_params=pltpu.CompilerParams(vmem_limit_bytes=VMEM_BYTES),
-        cost_estimate=pl.CostEstimate(flops=4 * 10**9, bytes_accessed=2 * 2**20, transcendentals=0),
         name="slot_terms",
-    )(blk, cel, cnt, om, feats, coords, mix, coef, lift)
+    )(*args)
 
 
 def modes_value(tag_col, tag_row, terms, z_hi, z_lo, xy):
@@ -178,84 +199,247 @@
     return out * (1.0 / math.sqrt(32768.0))
 
 
-def modes_kernel(tag_col, tag_row, terms, z_hi, z_lo, xy, out):
+def swap_rows_runs(x):
+    rows, lanes = x.shape
+    row = lax.broadcasted_iota(jnp.int32, x.shape, 0) % 8
+    run = (lax.broadcasted_iota(jnp.int32, x.shape, 1) % 128) // 16
+    for step in (1, 2, 4):
+        row_bit = (row // step) % 2
+        run_bit = (run // step) % 2
+        down = pltpu.roll(pltpu.roll(x, lanes - 16 * step, 1), step, 0)
+        up = pltpu.roll(pltpu.roll(x, 16 * step, 1), rows - step, 0)
+        x = jnp.where(row_bit == run_bit, x, jnp.where(row_bit == 1, down, up))
+    return x
+
+
+def exchange_kernel(
+    terms, tags, cot, z_hi, z_lo, xy, out,
+    terms_in, tags_in, cot_in, x_out, x_in, pick, g_out, g_in, fold,
+    t_send, t_recv, n_send, n_recv, c_send, c_recv, x_send, x_recv, g_send, g_recv,
+):
+    dp = lax.axis_index("dp")
+    slab = lax.axis_index("slab")
+    z = dp // 4
+    part = dp - z * 4
+
+    def copy_to(src, dst, send, recv, dp_to, slab_to):
+        return pltpu.make_async_remote_copy(
+            src_ref=src, dst_ref=dst, send_sem=send, recv_sem=recv,
+            device_id=(dp_to, slab_to), device_id_type=pl.DeviceIdType.MESH,
+        )
+
+    def terms_copy(to):
+        return copy_to(terms.at[to], terms_in.at[slab], t_send.at[to], t_recv.at[slab], dp, to)
+
+    def tags_copy(to):
+        return copy_to(tags, tags_in.at[slab], n_send.at[to], n_recv.at[slab], dp, to)
+
+    def cot_copy(to):
+        return copy_to(cot.at[lax.rem(to, 4)], cot_in.at[dp], c_send.at[to], c_recv.at[dp], to, slab)
+
+    def x_copy(to):
+        rows = pl.ds(pl.multiple_of(to * 8, 8), 8)
+        dp_to = slab * 4 + lax.rem(to, 4)
+        return copy_to(x_out.at[:, rows], x_in.at[dp], x_send.at[to], x_recv.at[dp], dp_to, to // 4)
+
+    def g_copy(to):
+        return copy_to(g_out.at[to], g_in.at[part], g_send.at[to], g_recv.at[part], z * 4 + to, slab)
+
+    own_x = slab * 4 + part
+    own_terms = pltpu.make_async_copy(terms.at[slab], terms_in.at[slab], t_recv.at[slab])
+    own_tags = pltpu.make_async_copy(tags, tags_in.at[slab], n_recv.at[slab])
+    own_cot = pltpu.make_async_copy(cot.at[part], cot_in.at[dp], c_recv.at[dp])
+    own_rows = pl.ds(pl.multiple_of(own_x * 8, 8), 8)
+    own_x_copy = pltpu.make_async_copy(x_out.at[:, own_rows], x_in.at[dp], x_recv.at[dp])
+    to_self = z == slab
+
+    def others(count, me, act):
+        def step(i, carry):
+            act(lax.rem(me + i, count))
+            return carry
+
+        lax.fori_loop(1, count, step, 0)
+
+    barrier = pltpu.get_barrier_semaphore()
+
+    def greet(dp_to, slab_to):
+        pl.semaphore_signal(
+            barrier, inc=1, device_id=(dp_to, slab_to), device_id_type=pl.DeviceIdType.MESH
+        )
+
+    others(8, slab, lambda to: greet(dp, to))
+    others(32, dp, lambda to: greet(to, slab))
+    others(32, dp, lambda to: greet(to, z))
+
+    @pl.when(jnp.logical_not(to_self))
+    def _():
+        greet(dp, z)
+
+    pl.semaphore_wait(barrier, 7 + 31 + 32 - to_self.astype(jnp.int32))
+
+    own_terms.start()
+    own_tags.start()
+    own_cot.start()
+
+    def start_slab(to):
+        terms_copy(to).start()
+        tags_copy(to).start()
+
+    others(8, slab, start_slab)
+    others(32, dp, lambda to: cot_copy(to).start())
+
+    own_terms.wait()
+    own_tags.wait()
+
+    def wait_slab(frm):
+        copy_to(terms.at[frm], terms_in.at[frm], t_send.at[frm], t_recv.at[frm], dp, frm).wait_recv()
+        copy_to(tags, tags_in.at[frm], n_send.at[frm], n_recv.at[frm], dp, frm).wait_recv()
+
+    others(8, slab, wait_slab)
     t = jnp.concatenate(
-        [jnp.concatenate([terms[r, e] for r in range(8)], axis=0) for e in range(8)], axis=1
+        [jnp.concatenate([terms_in[r, e] for r in range(8)], axis=0) for e in range(8)], axis=1
     )
-    col = jnp.concatenate([tag_col[...]] * 2, axis=1)
-    row = jnp.broadcast_to(tag_row[0:1, :], (256, 256))
-    out[...] = modes_value(col, row, t, z_hi[...], z_lo[...], xy[...]).astype(out.dtype)
-
-
-def kept_modes(tag_col, tag_row, terms):
+    tag_sum = tags_in[0]
+    for r in range(1, 8):
+        tag_sum = tag_sum + tags_in[r]
+    row = jnp.broadcast_to(tag_sum[0:1, :], (256, 256))
+    x = modes_value(row.T.astype(jnp.int32), row.astype(jnp.int32), t, z_hi[...], z_lo[...], xy[...])
+    x = swap_rows_runs(x)
+    x_out[0] = x[:, :128]
+    x_out[1] = x[:, 128:]
+
+    @pl.when(to_self)
+    def _():
+        own_x_copy.start()
+
+    @pl.when(jnp.logical_not(to_self))
+    def _():
+        x_copy(own_x).start()
+
+    others(32, own_x, lambda to: x_copy(to).start())
+    own_cot.wait()
+
+    def wait_cot(frm):
+        copy_to(cot.at[0], cot_in.at[frm], c_send.at[frm], c_recv.at[frm], frm, slab).wait_recv()
+
+    others(32, dp, wait_cot)
+
+    def wait_x(frm):
+        copy_to(x_out.at[:, pl.ds(0, 8)], x_in.at[frm], x_send.at[frm], x_recv.at[frm], frm, z).wait_recv()
+
+    others(32, dp, wait_x)
+
+    @pl.when(to_self)
+    def _():
+        own_x_copy.wait()
+
+    @pl.when(jnp.logical_not(to_self))
+    def _():
+        wait_x(dp)
+
+    def channels(to):
+        both = x_in[:, to // 2]
+        pick[...] = jnp.where(lax.rem(to, 2) == 1, pltpu.roll(both, 4, 1), both)
+        for o in range(4):
+            low = pl.ds(o * 16, 16)
+            high = pl.ds(64 + o * 16, 16)
+
+            def sample(s, acc):
+                g_low = cot_in[s, low, :].astype(F32)
+                g_high = cot_in[s, high, :].astype(F32)
+                new = []
+                for q in range(4):
+                    xq = pick[s, q : q + 1, :]
+                    new.append(acc[2 * q] + xq * g_low)
+                    new.append(acc[2 * q + 1] + xq * g_high)
+                return tuple(new)
+
+            acc = lax.fori_loop(0, 32, sample, tuple(jnp.zeros((16, 128), F32) for _ in range(8)), unroll=4)
+            for i in range(2):
+                re_low, re_high, im_low, im_high = acc[4 * i : 4 * i + 4]
+                fold[i, low, :] = re_low + im_high
+                fold[i, high, :] = re_high - im_low
+        for i in range(2):
+            g_out[to, i] = fold[i].T.astype(BF16)
+
+    def one(k, carry):
+        other = (1 - part // 2) * 2 + k
+        here = (part // 2) * 2 + lax.rem(part + k + 1, 2)
+        to = jnp.where(k < 2, other, here)
+        channels(to)
+
+        @pl.when(k < 3)
+        def _():
+            g_copy(to).start()
+
+        return carry
+
+    lax.fori_loop(0, 4, one, 0)
+    out[0, part] = g_out[part, 0]
+    out[1, part] = g_out[part, 1]
+
+    def take(frm):
+        copy_to(g_out.at[frm], g_in.at[frm], g_send.at[frm], g_recv.at[frm], z * 4 + frm, slab).wait_recv()
+        out[0, frm] = g_in[frm, 0]
+        out[1, frm] = g_in[frm, 1]
+
+    others(4, part, take)
+
+    def sent_slab(to):
+        terms_copy(to).wait_send()
+        tags_copy(to).wait_send()
+
+    others(8, slab, sent_slab)
+    others(32, dp, lambda to: cot_copy(to).wait_send())
+    others(32, own_x, lambda to: x_copy(to).wait_send())
+
+    @pl.when(jnp.logical_not(to_self))
+    def _():
+        x_copy(own_x).wait_send()
+
+    others(4, part, lambda to: g_copy(to).wait_send())
+
+
+def exchange(terms, tags, cot):
     z_hi, z_lo, xy = (jnp.asarray(t) for t in tables())
     vm = pl.BlockSpec(memory_space=pltpu.VMEM)
+    dma = pltpu.SemaphoreType.DMA
     return pl.pallas_call(
-        modes_kernel,
-        out_shape=jax.ShapeDtypeStruct((256, 256), BF16),
+        exchange_kernel,
+        out_shape=jax.ShapeDtypeStruct((2, 4, 128, 128), BF16),
         in_specs=[vm] * 6,
         out_specs=vm,
-        compiler_params=pltpu.CompilerParams(vmem_limit_bytes=VMEM_BYTES),
-        name="kept_modes",
-    )(tag_col, tag_row, terms, z_hi, z_lo, xy)
-
-
-def grad_kernel(x, g, out):
-    sign = jnp.where(lax.broadcasted_iota(jnp.int32, (16, 128), 1) < 64, 1.0, -1.0)
-
-    def mode_rows(k, carry):
-        xk = x[k].astype(F32)
-        rows = pl.ds(pl.multiple_of(k * 16, 16), 16)
-        acc = [jnp.zeros((16, 128), F32) for _ in range(4)]
-        for s in range(32):
-            gs = g[s, rows, :].astype(F32)
-            for q in range(4):
-                acc[q] = acc[q] + xk[q * 16 : (q + 1) * 16, s : s + 1] * gs
-        for i in range(2):
-            out[i, rows, :] = acc[2 * i] + sign * pltpu.roll(acc[2 * i + 1], 64, 1)
-        return carry
-
-    lax.fori_loop(0, 32, mode_rows, 0)
-
-
-def weight_grad(x, g):
-    vm = pl.BlockSpec(memory_space=pltpu.VMEM)
-    return pl.pallas_call(
-        grad_kernel,
-        out_shape=jax.ShapeDtypeStruct((2, 512, 128), F32),
-        in_specs=[vm] * 2,
-        out_specs=vm,
-        compiler_params=pltpu.CompilerParams(vmem_limit_bytes=VMEM_BYTES),
-        name="weight_grad",
-    )(x, g)
+        scratch_shapes=[
+            pltpu.VMEM((8, 8, 32, 128), BF16),
+            pltpu.VMEM((8, 8, 256), F32),
+            pltpu.VMEM((32, 128, 128), BF16),
+            pltpu.VMEM((2, 256, 128), F32),
+            pltpu.VMEM((32, 2, 8, 128), F32),
+            pltpu.VMEM((32, 8, 128), F32),
+            pltpu.VMEM((4, 2, 128, 128), BF16),
+            pltpu.VMEM((4, 2, 128, 128), BF16),
+            pltpu.VMEM((2, 128, 128), F32),
+            dma((8,)), dma((8,)), dma((8,)), dma((8,)), dma((32,)), dma((32,)),
+            dma((32,)), dma((32,)), dma((4,)), dma((4,)),
+        ],
+        compiler_params=pltpu.CompilerParams(
+            vmem_limit_bytes=VMEM_BYTES, collective_id=0, has_side_effects=True
+        ),
+        name="exchange",
+    )(terms, tags, cot, z_hi, z_lo, xy)
 
 
 def per_device(
     point_feats, point_coords, slot_block, slot_cell, slot_count, cotangent,
     offset_map, offset_bias, kernel_mix, lift_weight,
 ):
-    grads = cotangent[0].reshape(512, 128).astype(BF16)
-    grads_all = lax.all_gather(grads, "dp", axis=0, tiled=False)
-    cells = slot_cell[0, 0]
-    counts = slot_count[0, 0]
-    is_live = jnp.arange(4, dtype=jnp.int32)[None, :] < counts[:, None]
-    tags = jnp.where(is_live, jnp.arange(8, dtype=jnp.int32)[:, None] * 2048 + cells, -1).reshape(1, 32)
-    tags_in = lax.all_to_all(jnp.broadcast_to(tags, (8, 32)), "slab", 0, 0, tiled=True).reshape(256)
-    tag_col = jnp.broadcast_to(tags_in[:, None], (256, 128))
-    tag_row = jnp.broadcast_to(tags_in[None, :], (8, 256))
-    mix = jnp.transpose(kernel_mix, (0, 2, 1)).reshape(4096, 64)
-    coef = jnp.concatenate([offset_map, offset_bias[:, None]], axis=1)
-    terms = lifted_terms(
-        slot_block.reshape(32), slot_cell.reshape(32), counts, offset_map.reshape(192),
-        point_feats[0], point_coords[0], mix, coef, lift_weight.T,
+    terms, tags, cot = lifted_terms(
+        slot_block[0, 0], slot_cell[0, 0], slot_count[0, 0], offset_map,
+        point_feats[0], point_coords[0], kernel_mix, offset_map, offset_bias[:, None], lift_weight,
+        cotangent.reshape(512, 128),
     )
-    terms_in = lax.all_to_all(terms, "slab", 0, 0, tiled=True)
-    x = kept_modes(tag_col, tag_row, terms_in)
-    x = lax.all_to_all(x.reshape(8, 32, 256), "slab", 0, 0, tiled=True)
-    x = x.reshape(8, 32, 4, 64).transpose(0, 2, 1, 3).reshape(32, 32, 64)
-    x = lax.all_to_all(x, "dp", 0, 0, tiled=True)
-    grad = weight_grad(x.transpose(1, 2, 0), grads_all)
-    return grad.reshape(2, 2, 16, 16, 128)
+    grad = exchange(terms, tags, cot)
+    return grad.astype(F32).reshape(2, 2, 16, 16, 128)
 
 
 def solution(mesh):

time: 138 us -> 107 us (0.78)
  the two profiles are of different devices: /device:TPU:1 before, /device:TPU:25 now
where the time goes in v2:
time: 107 us; the launch traced here: 106 us
  Pallas kernels  99.9 us (93%)
  local copies, waits for them, and re-layouts  4.14 us (4%)
  other arithmetic  1.78 us (2%)
    pallas_call x1, Pallas kernels, exchange(): pl.pallas_call(exchange_kernel, out_shape=jax.ShapeDtypeStruct((2, 4, 128...  70.3 us
    pallas_call x1, Pallas kernels, lifted_terms(): pl.pallas_call(terms_kernel, out_shape=(jax.ShapeDtypeStruct((8, 8, 32, 1...  29.6 us

profile of v2, /device:TPU:25, one launch (start us, length us, event | category | flops | bytes accessed | tf_op | source)
XLA Modules:
  0.0 105.8 jit_solution(3133664422381402079)
XLA Ops:
  0.0 0.0 copy-start
  0.0 0.0 copy-start.1
  0.0 1.4 %copy.15.blk = s32[8,4]{1,0:T(8,128)} copy(s32[8,4]{0,1:T(4,128)} %bitcast.15) | data formatting | bytes 256 | tf_op jit(solution)/shard_map/squeeze | solution.py:437
  1.4 0.0 copy-done.1
  1.4 0.7 copy.16.cel
  2.0 0.0 copy-done
  2.0 0.0 copy-start.2
  2.1 0.6 copy.21
  2.7 0.1 copy-done.2
  2.7 0.0 copy-start.3
  2.7 0.7 copy.17.om.coef
  3.4 0.0 copy-done.3
  3.4 0.7 copy.19.bias_ref
  4.2 29.6 %slot_terms.1 = (bf16[8,8,32,128]{3,2,1,0:T(8,128)(2,1)}, f32[8,256]{1,0:T(8,128)}, bf16[4,128,128]{2,1,0:T(8,128)(2,1)}) custom-call(s32[8,4]{1,0:T(8,128)} %copy.15.blk, s32[8,4]{1,0:T(8,128)} %copy.16.cel, s32[8]{0:T(128)} %bitcast.17, f32[64,3]{1,0:T(8,128)} %copy.17.om.coef, bf16[16,64,128]{2,1,0:T(8,128)(2,1)} %bitcast.12, ...), custom_call_target="tpu_custom_call" | custom-call | tf_op jit(solution)/shard_map/slot_terms/pallas_call | solution.py:144
  33.7 70.3 %exchange.1 = bf16[2,4,128,128]{3,2,1,0:T(8,128)(2,1)} custom-call(bf16[8,8,32,128]{3,2,1,0:T(8,128)(2,1)} %get-tuple-element.8.terms, f32[8,256]{1,0:T(8,128)} %get-tuple-element.9.tags, bf16[4,128,128]{2,1,0:T(8,128)(2,1)} %get-tuple-element.10.cot, bf16[128,256]{1,0:T(8,128)(2,1)} %constant.6.clone.z_hi, bf16[128,256]{1,0:T(8,128)(2,1)} %constant.7.clone.z_lo, ...), custom_call_target="tpu_custom_call" | custom-call | tf_op jit(solution)/shard_map/exchange/pallas_call | solution.py:407
  104.1 1.8 %convert.1 = f32[2,2,16,16,128]{4,3,2,1,0:T(8,128)} convert(bf16[2,2,16,16,128]{4,3,2,1,0:T(8,128)(2,1)} %bitcast.11) | non-fusion elementwise | flops 131072 | bytes 786432 | tf_op jit(solution)/shard_map/reshape | solution.py:442
Async XLA Ops:
  0.0 2.0 %copy-start = (bf16[1,16,3,128]{3,1,2,0:T(8,128)(2,1)S(1)}, bf16[1,16,3,128]{3,1,2,0:T(8,128)(2,1)}, u32[]{:S(2)}) copy-start(bf16[1,16,3,128]{3,1,2,0:T(8,128)(2,1)} %param.14) | copy-start | bytes 36868
  0.0 1.4 %copy-start.1 = (s32[1,1,8,4]{2,3,1,0:T(4,128)S(1)}, s32[1,1,8,4]{2,3,1,0:T(4,128)}, u32[]{:S(2)}) copy-start(s32[1,1,8,4]{2,3,1,0:T(4,128)} %param.16) | copy-start | bytes 388
  2.0 0.7 copy-start.2
  2.7 0.7 copy-start.3
